TPU v7x, 32 devices: a whole 2x2x4 slice. The times are simulated.
32 devices in a mesh: sfc: 16 (over z, y, x), lev: 2 (over core).
Axes of the slice: x: 2, y: 2, z: 4, core: 2. Of those that a mesh axis runs over, the one named last changes fastest.
Arguments:
- air_state: float32 [24, 8, 32768], P(None, 'lev', 'sfc'), may hold values from -6 to 6
- metric: float32 [2, 2048], P(None, 'sfc'), may hold values from -5 to 5
- jacobian: float32 [2048], P('sfc'), may hold values from 0.25 to 4
- edge_nbr: int32 [4, 2048], P(None, 'sfc'), may hold values from 0 to 2047, as said below
- edge_side: int32 [4, 2048], P(None, 'sfc'), may hold values from 0 to 3
- coszen: float32 [32768], P('sfc'), may hold values from -1 to 1
- kappa_base: float32 [112], replicated, may hold values from 0.02 to 2
- band_kappa: float32 [112, 20], replicated, may hold values from 0.005 to 0.2
- solar_weight: float32 [112], replicated, may hold values from 0.5 to 2
- stretch_pos: int32 [32768], P('sfc'), may hold values from 0 to 32767, as said below
- stretch_src: int32 [32768], P('sfc'), may hold values from 0 to 32767, as said below
Outputs:
- new_state: float32 [24, 8, 32768], P(None, 'lev', 'sfc')
- surface_flux: float32 [32768], P(('sfc', 'lev'))
Inputs may be any that keep to these rules, and one draw needn't show every extreme that they name: edge_nbr[k, g] lies within 128 elements of g along the curve, cyclically over 2048 elements; that distance is reached. stretch_pos is a permutation of the columns and stretch_src its inverse; column c belongs to the stretch of device stretch_pos[c] // 2048; each device receives 2048 columns, at most 256 of them from one device, a bound reached in every draw; the columns that one device sends to one device take consecutive stretch positions. `stretch_src`: the inverse of stretch_pos.
All inputs are finite; a program needn't handle non-finite values.
Results may differ from a plain program's by a relative error of at most 0.0001.
Values sent between devices are 32-bit elements; how exact they have to be, the bound alone decides.
A program may use at most 64 MiB of HBM per device.

v0:
```python
import jax
import jax.numpy as jnp
import numpy as np
from jax import lax
from jax.sharding import PartitionSpec as P

NODES = 16
GBLOCK = 16
GLL_POINTS = np.array([-1.0, -1.0 / np.sqrt(5.0), 1.0 / np.sqrt(5.0), 1.0])
EDGE_NODES = np.array([[4, 8], [13, 14], [11, 7], [2, 1]], dtype=np.int32)
STEP_DYN = 0.2
DEPTH_UNIT = 0.05
HEAT_SCALE = 0.1
FLUX_SCALE = 0.02


def extended(cells, sides, width):
    for axis, dim in sides:
        count = lax.axis_size(axis)
        head = lax.slice_in_dim(cells, 0, width, axis=dim)
        tail = lax.slice_in_dim(cells, cells.shape[dim] - width, cells.shape[dim], axis=dim)
        cells = jnp.concatenate(
            [
                lax.ppermute(tail, axis, [(i, (i + 1) % count) for i in range(count)]),
                cells,
                lax.ppermute(head, axis, [((i + 1) % count, i) for i in range(count)]),
            ],
            axis=dim,
        )
    return cells


def derivative_numpy():
    spacing = GLL_POINTS[:, None] - GLL_POINTS[None, :]
    unit_diag = np.eye(4)
    safe_space = np.where(unit_diag > 0, 1.0, spacing)
    weights_row = np.prod(safe_space, axis=1)
    derivative = weights_row[:, None] / weights_row[None, :] / safe_space
    inverse_gap = np.where(unit_diag > 0, 0.0, 1.0 / safe_space)
    derivative = np.where(unit_diag > 0, inverse_gap.sum(axis=1)[:, None], derivative)
    return (np.kron(derivative, np.eye(4)), np.kron(np.eye(4), derivative))


def edge_tables():
    edge_flat = EDGE_NODES.reshape(-1)
    select_rows = np.zeros((8, 16))
    select_rows[np.arange(8), edge_flat] = 1.0
    keep_nodes = 1.0 - select_rows.sum(axis=0)
    return (select_rows, keep_nodes)


def advance(element_grid, metric, rows_i, rows_j, start):
    first_term = jnp.einsum("an,flne->flae", rows_i, element_grid, precision=lax.Precision.HIGHEST)
    second_term = jnp.einsum("an,flne->flae", rows_j, element_grid, precision=lax.Precision.HIGHEST)
    return start + STEP_DYN * (metric[0] * first_term + metric[1] * second_term)


def radiate(tracers, sun_angle, kappa_base, band_kappa, solar_weight):
    squares = tracers * tracers
    groups = kappa_base.shape[0] // GBLOCK
    level_count = tracers.shape[1]
    column_count = tracers.shape[2]

    def one_group(running, pieces):
        base_rate, rate_rows, bright = pieces
        absorb = (
            jnp.einsum("gt,tln->gln", rate_rows, squares, precision=lax.Precision.HIGHEST)
            + base_rate[:, None, None]
        )
        layer_depth = absorb * DEPTH_UNIT
        depth_above = jnp.cumsum(layer_depth, axis=1) - layer_depth
        heating = jnp.einsum(
            "g,gln->ln",
            bright,
            jnp.exp(-depth_above) * (1.0 - jnp.exp(-layer_depth)),
            precision=lax.Precision.HIGHEST,
        )
        ground = jnp.einsum(
            "g,gn->n",
            bright,
            jnp.exp(-(depth_above[:, -1] + layer_depth[:, -1])),
            precision=lax.Precision.HIGHEST,
        )
        return ((running[0] + heating, running[1] + ground), None)

    start_vals = (
        jnp.zeros((level_count, column_count), jnp.float32),
        jnp.zeros((column_count,), jnp.float32),
    )
    stacked = (
        kappa_base.reshape(groups, GBLOCK),
        band_kappa.reshape(groups, GBLOCK, -1),
        solar_weight.reshape(groups, GBLOCK),
    )
    (heating, ground), _ = lax.scan(one_group, start_vals, stacked)
    sun_height = jnp.maximum(sun_angle, 0.0)
    return (HEAT_SCALE * sun_height * heating, FLUX_SCALE * sun_height * ground)


def exchange_edges(edge_values, jacobian):
    elem_count = edge_values.shape[3]
    edge_rows = edge_values.reshape(-1, elem_count)
    edge_block = jnp.concatenate([edge_rows, jacobian[None, :]], axis=0)
    return extended(edge_block, (("sfc", 1),), elem_count)


def physics_levels(tracers, sun_angle, kappa_base, band_kappa, solar_weight):
    local_cols = tracers.shape[2]
    lev_devices = lax.axis_size("lev")
    part_cols = local_cols // lev_devices
    whole_column = lax.all_to_all(tracers, "lev", split_axis=2, concat_axis=1, tiled=True)
    sun_part = lax.dynamic_slice_in_dim(sun_angle, lax.axis_index("lev") * part_cols, part_cols)
    heating, ground = radiate(whole_column, sun_part, kappa_base, band_kappa, solar_weight)
    heat_back = lax.all_to_all(heating, "lev", split_axis=0, concat_axis=1, tiled=True)
    return (heat_back, ground)


def first_of_group(group_ids, values, group_count, sentinel):
    device_lane = jnp.arange(group_count, dtype=jnp.int32)
    member = group_ids[:, None] == device_lane[None, :]
    lowest = jnp.min(jnp.where(member, values[:, None], sentinel), axis=0)
    return values - jnp.sum(jnp.where(member, lowest[None, :], 0), axis=1)


def local(
    air_state,
    metric,
    jacobian,
    edge_nbr,
    edge_side,
    coszen,
    kappa_base,
    band_kappa,
    solar_weight,
    stretch_pos,
    stretch_src,
):
    field_count, level_count, local_cols = air_state.shape
    elem_count = local_cols // NODES
    table_i, table_j = derivative_numpy()
    select_np, keep_np = edge_tables()
    along_i = jnp.asarray(table_i, jnp.float32)
    along_j = jnp.asarray(table_j, jnp.float32)
    select_rows = jnp.asarray(select_np, jnp.float32)
    place_rows = jnp.asarray(select_np.T.copy(), jnp.float32)
    keep_nodes = jnp.asarray(keep_np, jnp.float32)
    element_grid = air_state.reshape(field_count, level_count, NODES, elem_count)
    advanced = advance(element_grid, metric, along_i, along_j, element_grid)
    edge_values = jnp.einsum(
        "an,flne->flae", select_rows, advanced, precision=lax.Precision.HIGHEST
    )
    padded = exchange_edges(edge_values, jacobian)
    sfc_devices = lax.axis_size("sfc")
    all_cols = local_cols * sfc_devices
    window_start = (lax.axis_index("sfc") - 1) * elem_count
    near_index = jnp.mod(edge_nbr - window_start, elem_count * sfc_devices)
    span_width = 3 * elem_count
    flip_pair = jnp.asarray(np.array([1, 0], dtype=np.int32))
    take_index = (2 * edge_side[:, None, :] + flip_pair[None, :, None]) * span_width + near_index[
        :, None, :
    ]
    far_rows = padded[:-1].reshape(field_count * level_count, 8 * span_width)
    far_values = jnp.take(far_rows, take_index.reshape(-1), axis=1).reshape(
        field_count, level_count, 8, elem_count
    )
    far_jac = jnp.take(padded[-1], near_index.reshape(-1)).reshape(4, 1, elem_count)
    far_jac = jnp.broadcast_to(far_jac, (4, 2, elem_count)).reshape(8, elem_count)
    summed = (jacobian * edge_values + far_jac * far_values) / (jacobian + far_jac)
    placed = jnp.einsum("ak,flke->flae", place_rows, summed, precision=lax.Precision.HIGHEST)
    dynamic = (advanced * keep_nodes[:, None] + placed).reshape(
        field_count, level_count, local_cols
    )
    capacity = 2 * local_cols // sfc_devices
    target_dev = stretch_pos // local_cols
    buffer_slot = first_of_group(target_dev, stretch_pos, sfc_devices, all_cols)
    flat_slot = target_dev * capacity + buffer_slot
    slot_column = (
        jnp.zeros((sfc_devices * capacity,), jnp.int32)
        .at[flat_slot]
        .set(jnp.arange(local_cols, dtype=jnp.int32))
    )
    source_dev = stretch_src // local_cols
    position_ids = jnp.arange(local_cols, dtype=jnp.int32)
    source_rank = first_of_group(source_dev, position_ids, sfc_devices, local_cols)
    recv_index = source_dev * capacity + source_rank
    tracer_count = field_count - 4
    tracer_rows = dynamic[4:].reshape(tracer_count * level_count, local_cols)
    sent_tracers = jnp.take(tracer_rows, slot_column, axis=1)
    sent_sun = jnp.take(coszen, slot_column)[None, :]
    got_tracers, got_sun = (
        lax.all_to_all(sent_tracers, "sfc", split_axis=1, concat_axis=1, tiled=True),
        lax.all_to_all(sent_sun, "sfc", split_axis=1, concat_axis=1, tiled=True),
    )
    stretch_tracers = jnp.take(got_tracers, recv_index, axis=1).reshape(
        tracer_count, level_count, local_cols
    )
    stretch_sun = jnp.take(got_sun[0], recv_index)
    heating, surface_flux = physics_levels(
        stretch_tracers, stretch_sun, kappa_base, band_kappa, solar_weight
    )
    position_of_slot = (
        jnp.zeros((sfc_devices * capacity,), jnp.int32).at[recv_index].set(position_ids)
    )
    returned = lax.all_to_all(
        jnp.take(heating, position_of_slot, axis=1), "sfc", split_axis=1, concat_axis=1, tiled=True
    )
    heat_cols = jnp.take(returned, flat_slot, axis=1)
    new_state = dynamic.at[2].add(heat_cols)
    return (new_state, surface_flux)


def solution(mesh):
    return jax.shard_map(
        local,
        mesh=mesh,
        in_specs=(
            P(None, "lev", "sfc"),
            P(None, "sfc"),
            P("sfc"),
            P(None, "sfc"),
            P(None, "sfc"),
            P("sfc"),
            P(),
            P(),
            P(),
            P("sfc"),
            P("sfc"),
        ),
        out_specs=(P(None, "lev", "sfc"), P(("sfc", "lev"))),
        check_vma=False,
    )
```

profile of v0, /device:TPU:0, one launch (start us, length us, event | category | flops | bytes accessed | tf_op | source)
XLA Modules:
  0.0 224.6 jit_solution(11954770912788300574)
XLA Ops:
  0.7 1.6 reshape.316
  2.3 0.8 convolution_multiply_fusion
  3.1 0.9 fusion.25
  4.6 3.0 %collective-permute-start = (f32[769,128]{1,0:T(8,128)S(1)}, f32[769,128]{1,0:T(8,128)S(1)}, u32[]{:S(2)}, u32[]{:S(2)}) collective-permute-start(f32[769,128]{1,0:T(8,128)S(1)} %pad_maximum_fusion.3), channel_id=1, source_target_pairs={{0,2},{2,4},{4,6},{6,8},{8,10},{10,12},{12,14},{14,16},{16,18},{18... | collective-permute-start | bytes 1181192 | tf_op jit(solution)/shard_map/ppermute | solution.py:24
  7.6 4.1 %collective-permute-start.1 = (f32[769,128]{1,0:T(8,128)S(1)}, f32[769,128]{1,0:T(8,128)S(1)}, u32[]{:S(2)}, u32[]{:S(2)}) collective-permute-start(f32[769,128]{1,0:T(8,128)S(1)} %pad_maximum_fusion.3), channel_id=1, source_target_pairs={{2,0},{4,2},{6,4},{8,6},{10,8},{12,10},{14,12},{16,14},{18,16},{20... | collective-permute-start | bytes 1181192 | tf_op jit(solution)/shard_map/ppermute | solution.py:26
  12.5 8.1 %scatter_custom_fusion.1 = s32[4096]{0:T(1024)S(1)} fusion(s32[2048]{0:T(1024)S(1)} %get-tuple-element.93, s32[2048]{0:T(1024)S(1)} %iota.18, s32[]{:T(128)} %constant.211.clone.1), kind=kCustom, calls=%fused_computation.97 | custom fusion | bytes 16388 | tf_op jit(solution)/shard_map/scatter | solution.py:180
  20.6 23.0 %gather_fusion.2 = f32[4096]{0:T(1024)S(1)} fusion(f32[2048]{0:T(1024)S(1)} %copy-done, s32[4096]{0:T(1024)S(1)} %fusion.40), kind=kCustom, calls=%fused_computation.2 | custom fusion | bytes 49152 | tf_op jit(solution)/shard_map/jit(_take)/gather | solution.py:189
  44.3 3.4 %all-to-all-start = ((f32[1,16,256]{2,0,1:T(1,128)}), f32[1,16,256]{2,0,1:T(1,128)S(1)}, u32[]{:S(2)}, u32[]{:S(2)}) async-start(f32[1,16,256]{2,0,1:T(1,128)} %bitcast.24), calls=%async_computation | async-start | bytes 32768 | tf_op jit(solution)/shard_map/all_to_all | solution.py:192
  48.1 3.5 %gather_fusion = f32[512]{0:T(512)S(1)} fusion(f32[384]{0:T(512)S(1)} %maximum_reduce_fusion, s32[1024]{0:T(1024)S(1)} %pad_clamp_fusion), kind=kCustom, calls=%fused_computation | custom fusion | bytes 6144 | tf_op jit(solution)/shard_map/jit(_take)/gather | solution.py:166
  51.7 1.1 pad_maximum_fusion
  52.8 1.2 reshape.319
  54.0 1.7 copy.77
  55.8 2.8 %gather_fusion.1 = f32[1024,96]{1,0:T(8,128)S(1)} fusion(f32[96,3072]{0,1:T(8,128)S(1)} %copy.77, s32[1024]{0:T(1024)S(1)} %broadcast_clamp_fusion.2), kind=kCustom, calls=%fused_computation.1 | custom fusion | bytes 790528 | tf_op jit(solution)/shard_map/jit(_take)/gather | solution.py:163
  59.3 0.8 fusion.26
  61.3 10.8 %gather_fusion.4 = f32[4096,80]{1,0:T(8,128)S(1)} fusion(f32[80,2048]{0,1:T(8,128)S(1)} %copy.80, s32[4096]{0:T(1024)S(1)} %fusion.40), kind=kCustom, calls=%fused_computation.4 | custom fusion | bytes 2637824 | tf_op jit(solution)/shard_map/jit(_take)/gather | solution.py:188
  72.1 1.7 copy.81
  73.8 2.5 %broadcast_select_fusion = f32[80,16,256]{2,0,1:T(8,128)} fusion(f32[80,16,256]{2,0,1:T(8,128)} %copy.81, pred[16,256]{1,0:T(8,128)(4,1)S(1)} %broadcast_in_dim.170), kind=kLoop, calls=%fused_computation.50 | loop fusion | flops 327680 | bytes 2625536 | tf_op jit(solution)/shard_map/jit(_take)/select_n | solution.py:188
  76.4 7.0 %all-to-all-start.1 = ((f32[80,16,256]{2,0,1:T(8,128)}), f32[80,16,256]{2,0,1:T(8,128)S(1)}, u32[]{:S(2)}, u32[]{:S(2)}) async-start(f32[80,16,256]{2,0,1:T(8,128)} %broadcast_select_fusion), calls=%async_computation.1 | async-start | bytes 2621440 | tf_op jit(solution)/shard_map/all_to_all | solution.py:191
  85.1 8.2 %scatter_custom_fusion = s32[4096]{0:T(1024)S(1)} fusion(s32[2048]{0:T(1024)S(1)} %get-tuple-element.97, s32[2048]{0:T(1024)S(1)} %iota.17, s32[]{:T(128)} %constant.211.clone.1), kind=kCustom, calls=%fused_computation.99 | custom fusion | bytes 16388 | tf_op jit(solution)/shard_map/scatter | solution.py:202
  94.0 11.8 %gather_fusion.3 = f32[2048]{0:T(1024)S(1)} fusion(f32[4096]{0:T(1024)S(1)} %bitcast.132, s32[2048]{0:T(1024)S(1)} %broadcast_clamp_fusion.1), kind=kCustom, calls=%fused_computation.3 | custom fusion | bytes 24576 | tf_op jit(solution)/shard_map/jit(_take)/gather | solution.py:197
  105.8 6.5 %all-to-all-done.1 = f32[80,16,256]{2,0,1:T(8,128)S(1)} async-done(((f32[80,16,256]{2,0,1:T(8,128)}), f32[80,16,256]{2,0,1:T(8,128)S(1)}, u32[]{:S(2)}, u32[]{:S(2)}) %all-to-all-start.1) | async-done | bytes 1310752 | tf_op jit(solution)/shard_map/all_to_all | solution.py:191
  112.3 0.8 copy.82
  113.1 5.5 %gather_fusion.5 = f32[2048,80]{1,0:T(8,128)S(1)} fusion(f32[80,4096]{0,1:T(8,128)S(1)} %bitcast.134, s32[2048]{0:T(1024)S(1)} %broadcast_clamp_fusion.1), kind=kCustom, calls=%fused_computation.5 | custom fusion | bytes 1318912 | tf_op jit(solution)/shard_map/jit(_take)/gather | solution.py:194
  119.5 3.2 %copy.84 = f32[20,4,2048]{0,1,2:T(4,128)} copy(f32[20,4,2048]{2,1,0:T(4,128)S(1)} %broadcast_select_fusion.1) | data formatting | bytes 1310720 | tf_op jit(solution)/shard_map/jit(_take)/select_n | solution.py:194
  122.6 7.2 %reshape.428 = f32[2,1,81920]{2,1,0:T(1,128)S(1)} reshape(f32[2048,4,20]{2,1,0:T(4,128)} %bitcast.135) | data formatting | bytes 1310720
  129.9 4.3 %all_to_all.52 = f32[2,1,81920]{2,1,0:T(1,128)S(1)} all-to-all(f32[2,1,81920]{2,1,0:T(1,128)S(1)} %reshape.428), channel_id=1, replica_groups=mesh['sfc'=16,'lev'=2] {'lev'}, dimensions={0} | all-to-all | bytes 1310720 | tf_op jit(solution)/shard_map/all_to_all | solution.py:111
  134.7 2.6 %reduce.4 = f32[2,81920]{1,0:T(2,128)S(1)} reduce(f32[2,1,81920]{2,1,0:T(1,128)S(1)} %all_to_all.52, f32[]{:T(128)} %broadcast.316), dimensions={1}, to_apply=%all_to_all.40.reduce_sub_computation | reduce | bytes 1310724 | tf_op jit(solution)/shard_map/all_to_all | solution.py:111
  137.3 8.0 %reshape.429 = f32[2048,4,20]{2,1,0:T(4,128)} reshape(f32[2,81920]{1,0:T(2,128)S(1)} %reduce.4) | data formatting | bytes 1310720
  145.3 3.9 %bitcast_multiply_fusion.1 = f32[20,4,2048]{0,1,2:T(4,128)} fusion(f32[2048,4,20]{2,1,0:T(4,128)} %reshape.429), kind=kLoop, calls=%fused_computation.129 | loop fusion | flops 163840 | bytes 1310720 | tf_op jit(solution)/shard_map/mul | solution.py:59
  149.2 3.5 %copy.85 = f32[20,2,4,1024]{3,0,2,1:T(8,128)S(1)} copy(f32[20,2,4,1024]{0,2,3,1:T(4,128)} %bitcast.136) | data formatting | bytes 1310720 | tf_op jit(solution)/shard_map/mul | solution.py:59
  152.7 29.1 %while.14 = (s32[]{:T(128)}, f32[8,1024]{1,0:T(8,128)S(1)}, f32[1024]{0:T(1024)S(1)}, f32[7,16]{1,0:T(8,128)S(1)}, f32[7,16,20]{2,1,0:T(8,128)S(1)}, /*index=5*/...) while((s32[]{:T(128)}, f32[8,1024]{1,0:T(8,128)S(1)}, f32[1024]{0:T(1024)S(1)}, ...), condition=%wide.region_8.9_spmd.clone, body=%wide.region_6.8_spmd.clone.sunk | while | flops 35112960 | bytes 3696376 | solution.py:95
  154.0 2.1 reduce-window_subtract_fusion.2
  156.9 0.7 fusion.82
  158.2 2.1 reduce-window_subtract_fusion.2
  162.3 2.1 reduce-window_subtract_fusion.2
  165.2 0.7 fusion.82
  166.5 2.1 reduce-window_subtract_fusion.2
  170.6 2.1 reduce-window_subtract_fusion.2
  173.5 0.7 fusion.82
  174.8 2.1 reduce-window_subtract_fusion.2
  178.9 2.1 reduce-window_subtract_fusion.2
  182.4 3.7 %all_to_all.53 = f32[2,4,1024]{2,1,0:T(4,128)S(1)} all-to-all(f32[2,4,1024]{2,1,0:T(4,128)S(1)} %all_to_all.41), channel_id=1, replica_groups=mesh['sfc'=16,'lev'=2] {'lev'}, dimensions={0} | all-to-all | bytes 65536 | tf_op jit(solution)/shard_map/all_to_all | solution.py:114
  186.6 14.1 %gather_fusion.6 = f32[4096,4]{1,0:T(8,128)} fusion(f32[4,2048]{0,1:T(8,128)S(1)} %bitcast.145, s32[4096]{0:T(1024)S(1)} %fusion.39), kind=kCustom, calls=%fused_computation.6 | custom fusion | bytes 147456 | tf_op jit(solution)/shard_map/jit(_take)/gather | solution.py:205
  200.7 2.2 copy.87
  203.6 6.4 %all-to-all-start.4 = ((f32[4,16,256]{2,0,1:T(4,128)}), f32[4,16,256]{2,0,1:T(4,128)S(1)}, u32[]{:S(2)}, u32[]{:S(2)}) async-start(f32[4,16,256]{2,0,1:T(4,128)} %broadcast_select_fusion.2), calls=%async_computation.4 | async-start | bytes 131072 | tf_op jit(solution)/shard_map/all_to_all | solution.py:204
  210.0 1.1 reshape.320
  211.1 6.3 %all-to-all-done.4 = f32[4,16,256]{2,0,1:T(4,128)S(1)} async-done(((f32[4,16,256]{2,0,1:T(4,128)}), f32[4,16,256]{2,0,1:T(4,128)S(1)}, u32[]{:S(2)}, u32[]{:S(2)}) %all-to-all-start.4) | async-done | bytes 65568 | tf_op jit(solution)/shard_map/all_to_all | solution.py:204
  218.1 5.5 %gather_fusion.7 = f32[2048,4]{1,0:T(8,128)S(1)} fusion(f32[4,4096]{0,1:T(8,128)S(1)} %bitcast.142, s32[2048]{0:T(1024)S(1)} %broadcast_clamp_fusion), kind=kCustom, calls=%fused_computation.7 | custom fusion | bytes 73728 | tf_op jit(solution)/shard_map/jit(_take)/gather | solution.py:207
  (148 shorter events, 22.8 us)
Async XLA Ops:
  0.6 19.9 %copy-start = (f32[2048]{0:T(1024)S(1)}, f32[2048]{0:T(1024)}, u32[]{:S(2)}) copy-start(f32[2048]{0:T(1024)} %param.26) | copy-start | bytes 24580
  0.6 1.6 copy-start.10
  0.7 2.4 %copy-start.13 = (f32[16,16,1,1]{1,0,3,2:T(8,128)S(1)}, f32[16,16,1,1]{1,0,3,2:T(8,128)}, u32[]{:S(2)}) copy-start(f32[16,16,1,1]{1,0,3,2:T(8,128)} %constant.237) | copy-start | bytes 3076
  0.7 1.6 copy-start.18
  3.1 0.9 copy-start.15
  3.1 1.4 copy-start.8
  4.0 7.7 %copy-start.4 = (s32[2048]{0:T(1024)S(1)}, s32[2048]{0:T(1024)}, u32[]{:S(2)}) copy-start(s32[2048]{0:T(1024)} %param.30) | copy-start | bytes 24580
  4.6 43.5 %collective-permute-start = (f32[769,128]{1,0:T(8,128)S(1)}, f32[769,128]{1,0:T(8,128)S(1)}, u32[]{:S(2)}, u32[]{:S(2)}) collective-permute-start(f32[769,128]{1,0:T(8,128)S(1)} %pad_maximum_fusion.3), channel_id=1, source_target_pairs={{0,2},{2,4},{4,6},{6,8},{8,10},{10,12},{12,14},{14,16},{16,18},{18... | collective-permute-start | bytes 1181192 | tf_op jit(solution)/shard_map/ppermute | solution.py:24
  7.6 40.5 %collective-permute-start.1 = (f32[769,128]{1,0:T(8,128)S(1)}, f32[769,128]{1,0:T(8,128)S(1)}, u32[]{:S(2)}, u32[]{:S(2)}) collective-permute-start(f32[769,128]{1,0:T(8,128)S(1)} %pad_maximum_fusion.3), channel_id=1, source_target_pairs={{2,0},{4,2},{6,4},{8,6},{10,8},{12,10},{14,12},{16,14},{18,16},{20... | collective-permute-start | bytes 1181192 | tf_op jit(solution)/shard_map/ppermute | solution.py:26
  20.6 27.1 %copy-start.11 = (s32[4,128]{1,0:T(4,128)S(1)}, s32[4,128]{1,0:T(4,128)}, u32[]{:S(2)}) copy-start(s32[4,128]{1,0:T(4,128)} %param.24) | copy-start | bytes 6148
  20.6 27.2 %copy-start.17 = (s32[4,128]{1,0:T(4,128)S(1)}, s32[4,128]{1,0:T(4,128)}, u32[]{:S(2)}) copy-start(s32[4,128]{1,0:T(4,128)} %param.25) | copy-start | bytes 6148
  20.6 27.2 %copy-start.16 = (s32[2]{0:T(128)S(1)}, s32[2]{0:T(128)}, u32[]{:S(2)}) copy-start(s32[2]{0:T(128)} %constant.236.clone) | copy-start | bytes 28
  44.3 32.1 %all-to-all-start = ((f32[1,16,256]{2,0,1:T(1,128)}), f32[1,16,256]{2,0,1:T(1,128)S(1)}, u32[]{:S(2)}, u32[]{:S(2)}) async-start(f32[1,16,256]{2,0,1:T(1,128)} %bitcast.24), calls=%async_computation | async-start | bytes 32768 | tf_op jit(solution)/shard_map/all_to_all | solution.py:192
  48.1 3.5 %copy-start.3 = (f32[769,128]{1,0:T(8,128)}, f32[769,128]{1,0:T(8,128)S(1)}, u32[]{:S(2)}) copy-start(f32[769,128]{1,0:T(8,128)S(1)} %collective-permute-done.1) | copy-start | bytes 1181188
  58.6 0.7 copy-start.14
  58.6 0.7 copy-start.21
  60.1 0.9 copy-start.1
  76.3 7.1 %copy-start.9 = (f32[112,20]{0,1:T(8,128)S(1)}, f32[112,20]{0,1:T(8,128)}, u32[]{:S(2)}) copy-start(f32[112,20]{0,1:T(8,128)} %param.28) | copy-start | bytes 26884
  76.3 7.2 %copy-start.19 = (f32[112]{0:T(128)S(1)}, f32[112]{0:T(128)}, u32[]{:S(2)}) copy-start(f32[112]{0:T(128)} %param.29) | copy-start | bytes 1348
  76.3 7.3 %copy-start.20 = (f32[112]{0:T(128)S(1)}, f32[112]{0:T(128)}, u32[]{:S(2)}) copy-start(f32[112]{0:T(128)} %param.27) | copy-start | bytes 1348
  76.3 7.9 %copy-start.5 = (s32[2048]{0:T(1024)S(1)}, s32[2048]{0:T(1024)}, u32[]{:S(2)}) copy-start(s32[2048]{0:T(1024)} %param.31) | copy-start | bytes 24580
  76.4 36.0 %all-to-all-start.1 = ((f32[80,16,256]{2,0,1:T(8,128)}), f32[80,16,256]{2,0,1:T(8,128)S(1)}, u32[]{:S(2)}, u32[]{:S(2)}) async-start(f32[80,16,256]{2,0,1:T(8,128)} %broadcast_select_fusion), calls=%async_computation.1 | async-start | bytes 2621440 | tf_op jit(solution)/shard_map/all_to_all | solution.py:191
  118.6 0.7 copy-start.7
  186.5 16.3 %copy-start.6 = (pred[16,256]{1,0:T(8,128)(4,1)S(1)}, pred[16,256]{1,0:T(8,128)(4,1)}, u32[]{:S(2)}) copy-start(pred[16,256]{1,0:T(8,128)(4,1)} %broadcast_in_dim.162) | copy-start | bytes 12292
  186.6 23.4 %copy-start.2 = (f32[24,4,16,128]{3,2,1,0:T(8,128)S(1)}, f32[24,4,16,128]{3,2,1,0:T(8,128)}, u32[]{:S(2)}) copy-start(f32[24,4,16,128]{3,2,1,0:T(8,128)} %copy-done.1) | copy-start | bytes 2359300
  200.7 10.4 %slice-start = ((f32[24,4,16,128]{3,2,1,0:T(8,128)}), f32[1,4,16,128]{3,2,1,0:T(8,128)S(1)}, s32[]{:S(2)}) async-start(f32[24,4,16,128]{3,2,1,0:T(8,128)} %copy-done.1), calls=%async_computation.5 | async-start | bytes 65536 | tf_op jit(solution)/shard_map/slice.28
  203.6 13.9 %all-to-all-start.4 = ((f32[4,16,256]{2,0,1:T(4,128)}), f32[4,16,256]{2,0,1:T(4,128)S(1)}, u32[]{:S(2)}, u32[]{:S(2)}) async-start(f32[4,16,256]{2,0,1:T(4,128)} %broadcast_select_fusion.2), calls=%async_computation.4 | async-start | bytes 131072 | tf_op jit(solution)/shard_map/all_to_all | solution.py:204
  211.1 12.8 %copy-start.12 = (pred[2048]{0:T(1024)(128)(4,1)S(1)}, pred[2048]{0:T(1024)(128)(4,1)}, u32[]{:S(2)}) copy-start(pred[2048]{0:T(1024)(128)(4,1)} %get-tuple-element.92) | copy-start | bytes 6148
where the time goes:
time: 226 us; the launch traced here: 225 us
  local copies, waits for them, and re-layouts  136 us (60%)
  other arithmetic  30 us (13%)
  starting transfers between devices  23.9 us (11%)
  waiting for transfers between devices  12.9 us (6%)
  matrix products  11.6 us (5%)
  blocking collectives  8.01 us (4%)
    gather x1, local copies, waits for them, and re-layouts, local(): sent_sun = jnp.take(coszen, slot_column)[None, :]  23 us
    unnamed x49, local copies, waits for them, and re-layouts  16.8 us
    gather x2, local copies, waits for them, and re-layouts, local(): jnp.take(heating, position_of_slot, axis=1)  16.3 us
    another operation x7, other arithmetic, one_group(): depth_above = jnp.cumsum(layer_depth, axis=1) - layer_depth  15 us
    gather x2, local copies, waits for them, and re-layouts, local(): sent_tracers = jnp.take(tracer_rows, slot_column, axis=1)  12.5 us
    gather x1, local copies, waits for them, and re-layouts, local(): stretch_sun = jnp.take(got_sun[0], recv_index)  11.8 us
    scatter x1, local copies, waits for them, and re-layouts, local(): jnp.zeros((sfc_devices * capacity,), jnp.int32).at[recv_index]  8.24 us
    scatter x1, local copies, waits for them, and re-layouts, local(): slot_column = jnp.zeros((sfc_devices * capacity,), jnp.int32).at[flat_slo...  8.06 us
  transfers between devices with their start and end apart: 5, of which 2 were waited for; matrix products, arithmetic and copies ran while one was open for 37% of the time, Pallas kernels for 0%

commit v1 on v0

--- a/solution.py
+++ b/solution.py
@@ -201,9 +201,10 @@
     position_of_slot = (
         jnp.zeros((sfc_devices * capacity,), jnp.int32).at[recv_index].set(position_ids)
     )
-    returned = lax.all_to_all(
-        jnp.take(heating, position_of_slot, axis=1), "sfc", split_axis=1, concat_axis=1, tiled=True
-    )
+    own = jnp.take(heating, position_of_slot, axis=1)
+    shards = jnp.split(own, lax.axis_size("sfc"), axis=1)
+    incoming = lax.all_to_all(jnp.stack(shards), "sfc", 0, 0)
+    returned = jnp.concatenate(incoming, axis=1)
     heat_cols = jnp.take(returned, flat_slot, axis=1)
     new_state = dynamic.at[2].add(heat_cols)
     return (new_state, surface_flux)

time: 226 us -> 233 us (1.031)
  waiting for transfers between devices: 12.9 us -> 22 us
  local copies, waits for them, and re-layouts: 136 us -> 132 us
    all_to_all x1, waiting for transfers between devices: 6.53 us -> 15.6 us  [local(): lax.all_to_all(sent_tracers, 'sfc', split_axis=1, concat_axis=1, tiled=True)]
    gather x2 -> x1, local copies, waits for them, and re-layouts: 16.3 us -> 10.8 us  [local(): own = jnp.take(heating, position_of_slot, axis=1)]
    unnamed x49 -> x68, local copies, waits for them, and re-layouts: 16.8 us -> 16.7 us
  transfers between devices with their start and end apart: 5 -> 5, of which waited for: 2 -> 2; matrix products, arithmetic and copies ran while one was open for 37% -> 36% of each run, Pallas kernels for 0% -> 0%
where the time goes in v1:
time: 233 us; the launch traced here: 232 us
  local copies, waits for them, and re-layouts  132 us (57%)
  other arithmetic  32.2 us (14%)
  starting transfers between devices  23.8 us (10%)
  waiting for transfers between devices  22 us (9%)
  matrix products  12.3 us (5%)
  blocking collectives  8.01 us (3%)
    gather x1, local copies, waits for them, and re-layouts, local(): sent_sun = jnp.take(coszen, slot_column)[None, :]  23 us
    unnamed x68, local copies, waits for them, and re-layouts  16.7 us
    all_to_all x1, waiting for transfers between devices, local(): lax.all_to_all(sent_tracers, 'sfc', split_axis=1, concat_axis=1, tiled=True)  15.6 us
    another operation x7, other arithmetic, one_group(): depth_above = jnp.cumsum(layer_depth, axis=1) - layer_depth  15 us
    gather x2, local copies, waits for them, and re-layouts, local(): sent_tracers = jnp.take(tracer_rows, slot_column, axis=1)  12.5 us
    gather x1, local copies, waits for them, and re-layouts, local(): stretch_sun = jnp.take(got_sun[0], recv_index)  11.8 us
    gather x1, local copies, waits for them, and re-layouts, local(): own = jnp.take(heating, position_of_slot, axis=1)  10.8 us
    scatter x1, local copies, waits for them, and re-layouts, local(): slot_column = jnp.zeros((sfc_devices * capacity,), jnp.int32).at[flat_slo...  8.06 us
  transfers between devices with their start and end apart: 5, of which 2 were waited for; matrix products, arithmetic and copies ran while one was open for 36% of the time, Pallas kernels for 0%

profile of v1, /device:TPU:0, one launch (start us, length us, event | category | flops | bytes accessed | tf_op | source)
XLA Modules:
  0.0 232.2 jit_solution(16023395014770243272)
XLA Ops:
  0.7 1.5 reshape.314
  2.2 0.8 slice_bitcast_fusion.17
  3.0 1.5 convolution_multiply_fusion
  4.5 0.9 fusion.25
  6.0 3.0 %collective-permute-start = (f32[769,128]{1,0:T(8,128)S(1)}, f32[769,128]{1,0:T(8,128)S(1)}, u32[]{:S(2)}, u32[]{:S(2)}) collective-permute-start(f32[769,128]{1,0:T(8,128)S(1)} %pad_maximum_fusion.3), channel_id=1, source_target_pairs={{0,2},{2,4},{4,6},{6,8},{8,10},{10,12},{12,14},{14,16},{16,18},{18... | collective-permute-start | bytes 1181192 | tf_op jit(solution)/shard_map/ppermute | solution.py:24
  9.0 4.1 %collective-permute-start.1 = (f32[769,128]{1,0:T(8,128)S(1)}, f32[769,128]{1,0:T(8,128)S(1)}, u32[]{:S(2)}, u32[]{:S(2)}) collective-permute-start(f32[769,128]{1,0:T(8,128)S(1)} %pad_maximum_fusion.3), channel_id=1, source_target_pairs={{2,0},{4,2},{6,4},{8,6},{10,8},{12,10},{14,12},{16,14},{18,16},{20... | collective-permute-start | bytes 1181192 | tf_op jit(solution)/shard_map/ppermute | solution.py:26
  14.8 8.1 %scatter_custom_fusion = s32[4096]{0:T(1024)S(1)} fusion(s32[2048]{0:T(1024)S(1)} %get-tuple-element.97, s32[2048]{0:T(1024)S(1)} %iota.17, s32[]{:T(128)} %constant.211.clone.1), kind=kCustom, calls=%fused_computation.131 | custom fusion | bytes 16388 | tf_op jit(solution)/shard_map/scatter | solution.py:202
  22.9 8.1 %scatter_custom_fusion.1 = s32[4096]{0:T(1024)S(1)} fusion(s32[2048]{0:T(1024)S(1)} %get-tuple-element.93, s32[2048]{0:T(1024)S(1)} %iota.18, s32[]{:T(128)} %constant.211.clone.1), kind=kCustom, calls=%fused_computation.129 | custom fusion | bytes 16388 | tf_op jit(solution)/shard_map/scatter | solution.py:180
  31.0 23.0 %gather_fusion.2 = f32[4096]{0:T(1024)S(1)} fusion(f32[2048]{0:T(1024)S(1)} %copy-done, s32[4096]{0:T(1024)S(1)} %get-tuple-element.103), kind=kCustom, calls=%fused_computation.2 | custom fusion | bytes 49152 | tf_op jit(solution)/shard_map/jit(_take)/gather | solution.py:189
  54.6 3.5 %all-to-all-start = ((f32[1,16,256]{2,0,1:T(1,128)}), f32[1,16,256]{2,0,1:T(1,128)S(1)}, u32[]{:S(2)}, u32[]{:S(2)}) async-start(f32[1,16,256]{2,0,1:T(1,128)} %bitcast.24), calls=%async_computation | async-start | bytes 32768 | tf_op jit(solution)/shard_map/all_to_all | solution.py:192
  58.6 3.5 %gather_fusion = f32[512]{0:T(512)S(1)} fusion(f32[384]{0:T(512)S(1)} %maximum_reduce_fusion, s32[1024]{0:T(1024)S(1)} %pad_clamp_fusion), kind=kCustom, calls=%fused_computation | custom fusion | bytes 6144 | tf_op jit(solution)/shard_map/jit(_take)/gather | solution.py:166
  62.1 1.1 pad_maximum_fusion
  63.2 1.2 reshape.317
  64.5 1.7 copy.109
  66.2 2.8 %gather_fusion.1 = f32[1024,96]{1,0:T(8,128)S(1)} fusion(f32[96,3072]{0,1:T(8,128)S(1)} %copy.109, s32[1024]{0:T(1024)S(1)} %broadcast_clamp_fusion.2), kind=kCustom, calls=%fused_computation.1 | custom fusion | bytes 790528 | tf_op jit(solution)/shard_map/jit(_take)/gather | solution.py:163
  69.3 0.8 fusion.26
  71.4 10.8 %gather_fusion.4 = f32[4096,80]{1,0:T(8,128)S(1)} fusion(f32[80,2048]{0,1:T(8,128)S(1)} %copy.112, s32[4096]{0:T(1024)S(1)} %get-tuple-element.103), kind=kCustom, calls=%fused_computation.4 | custom fusion | bytes 2637824 | tf_op jit(solution)/shard_map/jit(_take)/gather | solution.py:188
  82.2 1.7 copy.113
  83.9 2.6 %broadcast_select_fusion = f32[80,16,256]{2,0,1:T(8,128)} fusion(f32[80,16,256]{2,0,1:T(8,128)} %copy.113, pred[16,256]{1,0:T(8,128)(4,1)S(1)} %broadcast_in_dim.167), kind=kLoop, calls=%fused_computation.51 | loop fusion | flops 327680 | bytes 2625536 | tf_op jit(solution)/shard_map/jit(_take)/select_n | solution.py:188
  86.5 6.9 %all-to-all-start.1 = ((f32[80,16,256]{2,0,1:T(8,128)}), f32[80,16,256]{2,0,1:T(8,128)S(1)}, u32[]{:S(2)}, u32[]{:S(2)}) async-start(f32[80,16,256]{2,0,1:T(8,128)} %broadcast_select_fusion), calls=%async_computation.1 | async-start | bytes 2621440 | tf_op jit(solution)/shard_map/all_to_all | solution.py:191
  94.9 11.8 %gather_fusion.3 = f32[2048]{0:T(1024)S(1)} fusion(f32[4096]{0:T(1024)S(1)} %bitcast.196, s32[2048]{0:T(1024)S(1)} %broadcast_clamp_fusion.1), kind=kCustom, calls=%fused_computation.3 | custom fusion | bytes 24576 | tf_op jit(solution)/shard_map/jit(_take)/gather | solution.py:197
  106.6 15.6 %all-to-all-done.1 = f32[80,16,256]{2,0,1:T(8,128)S(1)} async-done(((f32[80,16,256]{2,0,1:T(8,128)}), f32[80,16,256]{2,0,1:T(8,128)S(1)}, u32[]{:S(2)}, u32[]{:S(2)}) %all-to-all-start.1) | async-done | bytes 1310752 | tf_op jit(solution)/shard_map/all_to_all | solution.py:191
  122.3 0.8 copy.114
  123.1 5.5 %gather_fusion.5 = f32[2048,80]{1,0:T(8,128)S(1)} fusion(f32[80,4096]{0,1:T(8,128)S(1)} %bitcast.198, s32[2048]{0:T(1024)S(1)} %broadcast_clamp_fusion.1), kind=kCustom, calls=%fused_computation.5 | custom fusion | bytes 1318912 | tf_op jit(solution)/shard_map/jit(_take)/gather | solution.py:194
  129.5 3.2 %copy.116 = f32[20,4,2048]{0,1,2:T(4,128)} copy(f32[20,4,2048]{2,1,0:T(4,128)S(1)} %broadcast_select_fusion.1) | data formatting | bytes 1310720 | tf_op jit(solution)/shard_map/jit(_take)/select_n | solution.py:194
  132.6 7.2 %reshape.428 = f32[2,1,81920]{2,1,0:T(1,128)S(1)} reshape(f32[2048,4,20]{2,1,0:T(4,128)} %bitcast.199) | data formatting | bytes 1310720
  139.9 4.3 %all_to_all.48 = f32[2,1,81920]{2,1,0:T(1,128)S(1)} all-to-all(f32[2,1,81920]{2,1,0:T(1,128)S(1)} %reshape.428), channel_id=1, replica_groups=mesh['sfc'=16,'lev'=2] {'lev'}, dimensions={0} | all-to-all | bytes 1310720 | tf_op jit(solution)/shard_map/all_to_all | solution.py:111
  144.7 2.7 %reduce.4 = f32[2,81920]{1,0:T(2,128)S(1)} reduce(f32[2,1,81920]{2,1,0:T(1,128)S(1)} %all_to_all.48, f32[]{:T(128)} %broadcast.319), dimensions={1}, to_apply=%all_to_all.37.reduce_sub_computation | reduce | bytes 1310724 | tf_op jit(solution)/shard_map/all_to_all | solution.py:111
  147.4 8.0 %reshape.429 = f32[2048,4,20]{2,1,0:T(4,128)} reshape(f32[2,81920]{1,0:T(2,128)S(1)} %reduce.4) | data formatting | bytes 1310720
  155.4 3.9 %bitcast_multiply_fusion.1 = f32[20,4,2048]{0,1,2:T(4,128)} fusion(f32[2048,4,20]{2,1,0:T(4,128)} %reshape.429), kind=kLoop, calls=%fused_computation.161 | loop fusion | flops 163840 | bytes 1310720 | tf_op jit(solution)/shard_map/mul | solution.py:59
  159.3 3.5 %copy.117 = f32[20,2,4,1024]{3,0,2,1:T(8,128)S(1)} copy(f32[20,2,4,1024]{0,2,3,1:T(4,128)} %bitcast.200) | data formatting | bytes 1310720 | tf_op jit(solution)/shard_map/mul | solution.py:59
  162.8 29.1 %while.14 = (s32[]{:T(128)}, f32[8,1024]{1,0:T(8,128)S(1)}, f32[1024]{0:T(1024)S(1)}, f32[7,16]{1,0:T(8,128)S(1)}, f32[7,16,20]{2,1,0:T(8,128)S(1)}, /*index=5*/...) while((s32[]{:T(128)}, f32[8,1024]{1,0:T(8,128)S(1)}, f32[1024]{0:T(1024)S(1)}, ...), condition=%wide.region_8.9_spmd.clone, body=%wide.region_6.8_spmd.clone.sunk | while | flops 35112960 | bytes 3696376 | solution.py:95
  164.1 2.1 reduce-window_subtract_fusion.2
  167.0 0.7 fusion.98
  168.3 2.1 reduce-window_subtract_fusion.2
  172.4 2.1 reduce-window_subtract_fusion.2
  176.6 2.1 reduce-window_subtract_fusion.2
  180.7 2.1 reduce-window_subtract_fusion.2
  184.9 2.1 reduce-window_subtract_fusion.2
  189.1 2.1 reduce-window_subtract_fusion.2
  192.6 3.7 %all_to_all.49 = f32[2,4,1024]{2,1,0:T(4,128)S(1)} all-to-all(f32[2,4,1024]{2,1,0:T(4,128)S(1)} %all_to_all.38), channel_id=1, replica_groups=mesh['sfc'=16,'lev'=2] {'lev'}, dimensions={0} | all-to-all | bytes 65536 | tf_op jit(solution)/shard_map/all_to_all | solution.py:114
  196.7 10.8 %gather_fusion.6 = f32[4096,4]{1,0:T(8,128)S(1)} fusion(f32[4,2048]{0,1:T(8,128)S(1)} %bitcast.209, s32[4096]{0:T(1024)S(1)} %get-tuple-element.102), kind=kCustom, calls=%fused_computation.6 | custom fusion | bytes 147456 | tf_op jit(solution)/shard_map/jit(_take)/gather | solution.py:204
  207.5 2.1 select_bitcast_fusion
  210.0 1.2 copy.119
  211.2 6.4 %all-to-all-start.4 = ((f32[16,4,256]{2,1,0:T(4,128)}), f32[16,4,256]{2,1,0:T(4,128)S(1)}, u32[]{:S(2)}, u32[]{:S(2)}) async-start(f32[16,4,256]{2,1,0:T(4,128)} %copy.119), calls=%async_computation.4 | async-start | bytes 131072 | tf_op jit(solution)/shard_map/all_to_all | solution.py:206
  217.6 1.1 reshape.318
  218.8 6.3 %all-to-all-done.4 = f32[16,4,256]{2,1,0:T(4,128)S(1)} async-done(((f32[16,4,256]{2,1,0:T(4,128)}), f32[16,4,256]{2,1,0:T(4,128)S(1)}, u32[]{:S(2)}, u32[]{:S(2)}) %all-to-all-start.4) | async-done | bytes 65568 | tf_op jit(solution)/shard_map/all_to_all | solution.py:206
  225.8 5.5 %gather_fusion.7 = f32[2048,4]{1,0:T(8,128)S(1)} fusion(f32[4,4096]{0,1:T(8,128)S(1)} %bitcast.206, s32[2048]{0:T(1024)S(1)} %broadcast_clamp_fusion), kind=kCustom, calls=%fused_computation.7 | custom fusion | bytes 73728 | tf_op jit(solution)/shard_map/jit(_take)/gather | solution.py:208
  (166 shorter events, 23.4 us)
Async XLA Ops:
  0.6 30.3 %copy-start = (f32[2048]{0:T(1024)S(1)}, f32[2048]{0:T(1024)}, u32[]{:S(2)}) copy-start(f32[2048]{0:T(1024)} %param.26) | copy-start | bytes 24580
  0.6 3.8 %copy-start.16 = (f32[16,16,1,1]{1,0,3,2:T(8,128)S(1)}, f32[16,16,1,1]{1,0,3,2:T(8,128)}, u32[]{:S(2)}) copy-start(f32[16,16,1,1]{1,0,3,2:T(8,128)} %constant.237) | copy-start | bytes 3076
  2.2 3.2 %copy-start.18 = (f32[8,16,1,1]{1,0,3,2:T(8,128)S(1)}, f32[8,16,1,1]{1,0,3,2:T(8,128)}, u32[]{:S(2)}) copy-start(f32[8,16,1,1]{1,0,3,2:T(8,128)} %constant.239) | copy-start | bytes 1540
  4.5 1.5 copy-start.12
  4.5 8.6 %copy-start.5 = (s32[2048]{0:T(1024)S(1)}, s32[2048]{0:T(1024)}, u32[]{:S(2)}) copy-start(s32[2048]{0:T(1024)} %param.31) | copy-start | bytes 24580
  4.5 9.4 %copy-start.4 = (s32[2048]{0:T(1024)S(1)}, s32[2048]{0:T(1024)}, u32[]{:S(2)}) copy-start(s32[2048]{0:T(1024)} %param.30) | copy-start | bytes 24580
  6.0 52.6 %collective-permute-start = (f32[769,128]{1,0:T(8,128)S(1)}, f32[769,128]{1,0:T(8,128)S(1)}, u32[]{:S(2)}, u32[]{:S(2)}) collective-permute-start(f32[769,128]{1,0:T(8,128)S(1)} %pad_maximum_fusion.3), channel_id=1, source_target_pairs={{0,2},{2,4},{4,6},{6,8},{8,10},{10,12},{12,14},{14,16},{16,18},{18... | collective-permute-start | bytes 1181192 | tf_op jit(solution)/shard_map/ppermute | solution.py:24
  9.0 49.5 %collective-permute-start.1 = (f32[769,128]{1,0:T(8,128)S(1)}, f32[769,128]{1,0:T(8,128)S(1)}, u32[]{:S(2)}, u32[]{:S(2)}) collective-permute-start(f32[769,128]{1,0:T(8,128)S(1)} %pad_maximum_fusion.3), channel_id=1, source_target_pairs={{2,0},{4,2},{6,4},{8,6},{10,8},{12,10},{14,12},{16,14},{18,16},{20... | collective-permute-start | bytes 1181192 | tf_op jit(solution)/shard_map/ppermute | solution.py:26
  13.9 8.9 %copy-start.8 = (s32[2048]{0:T(1024)}, s32[2048]{0:T(1024)S(1)}, u32[]{:S(2)}) copy-start(s32[2048]{0:T(1024)S(1)} %get-tuple-element.97) | copy-start | bytes 24580
  14.8 39.3 %copy-start.6 = (s32[2048]{0:T(1024)}, s32[2048]{0:T(1024)S(1)}, u32[]{:S(2)}) copy-start(s32[2048]{0:T(1024)S(1)} %get-tuple-element.93) | copy-start | bytes 24580
  30.9 27.2 %copy-start.14 = (s32[4,128]{1,0:T(4,128)S(1)}, s32[4,128]{1,0:T(4,128)}, u32[]{:S(2)}) copy-start(s32[4,128]{1,0:T(4,128)} %param.24) | copy-start | bytes 6148
  31.0 27.2 %copy-start.20 = (s32[4,128]{1,0:T(4,128)S(1)}, s32[4,128]{1,0:T(4,128)}, u32[]{:S(2)}) copy-start(s32[4,128]{1,0:T(4,128)} %param.25) | copy-start | bytes 6148
  31.0 27.2 %copy-start.19 = (s32[2]{0:T(128)S(1)}, s32[2]{0:T(128)}, u32[]{:S(2)}) copy-start(s32[2]{0:T(128)} %constant.236.clone) | copy-start | bytes 28
  54.6 31.8 %all-to-all-start = ((f32[1,16,256]{2,0,1:T(1,128)}), f32[1,16,256]{2,0,1:T(1,128)S(1)}, u32[]{:S(2)}, u32[]{:S(2)}) async-start(f32[1,16,256]{2,0,1:T(1,128)} %bitcast.24), calls=%async_computation | async-start | bytes 32768 | tf_op jit(solution)/shard_map/all_to_all | solution.py:192
  58.5 3.6 %copy-start.3 = (f32[769,128]{1,0:T(8,128)}, f32[769,128]{1,0:T(8,128)S(1)}, u32[]{:S(2)}) copy-start(f32[769,128]{1,0:T(8,128)S(1)} %collective-permute-done.1) | copy-start | bytes 1181188
  66.2 3.1 %copy-start.17 = (f32[16,8,1,1]{0,1,3,2:T(8,128)S(1)}, f32[16,8,1,1]{0,1,3,2:T(8,128)}, u32[]{:S(2)}) copy-start(f32[16,8,1,1]{0,1,3,2:T(8,128)} %constant.240) | copy-start | bytes 1540
  66.2 3.1 %copy-start.23 = (f32[16]{0:T(128)S(1)}, f32[16]{0:T(128)}, u32[]{:S(2)}) copy-start(f32[16]{0:T(128)} %constant.235.clone) | copy-start | bytes 196
  70.2 0.9 copy-start.1
  83.9 9.5 %copy-start.13 = (f32[112,20]{0,1:T(8,128)S(1)}, f32[112,20]{0,1:T(8,128)}, u32[]{:S(2)}) copy-start(f32[112,20]{0,1:T(8,128)} %param.28) | copy-start | bytes 26884
  83.9 9.6 %copy-start.21 = (f32[112]{0:T(128)S(1)}, f32[112]{0:T(128)}, u32[]{:S(2)}) copy-start(f32[112]{0:T(128)} %param.29) | copy-start | bytes 1348
  83.9 9.7 %copy-start.22 = (f32[112]{0:T(128)S(1)}, f32[112]{0:T(128)}, u32[]{:S(2)}) copy-start(f32[112]{0:T(128)} %param.27) | copy-start | bytes 1348
  83.9 10.4 %copy-start.9 = (s32[2048]{0:T(1024)S(1)}, s32[2048]{0:T(1024)}, u32[]{:S(2)}) copy-start(s32[2048]{0:T(1024)} %copy-done.8) | copy-start | bytes 24580
  86.5 35.8 %all-to-all-start.1 = ((f32[80,16,256]{2,0,1:T(8,128)}), f32[80,16,256]{2,0,1:T(8,128)S(1)}, u32[]{:S(2)}, u32[]{:S(2)}) async-start(f32[80,16,256]{2,0,1:T(8,128)} %broadcast_select_fusion), calls=%async_computation.1 | async-start | bytes 2621440 | tf_op jit(solution)/shard_map/all_to_all | solution.py:191
  128.6 0.7 copy-start.11
  162.8 44.6 %copy-start.10 = (pred[4096]{0:T(1024)(128)(4,1)S(1)}, pred[4096]{0:T(1024)(128)(4,1)}, u32[]{:S(2)}) copy-start(pred[4096]{0:T(1024)(128)(4,1)} %compare_and_fusion.1) | copy-start | bytes 12292
  209.8 7.8 %copy-start.7 = (s32[2048]{0:T(1024)S(1)}, s32[2048]{0:T(1024)}, u32[]{:S(2)}) copy-start(s32[2048]{0:T(1024)} %copy-done.6) | copy-start | bytes 24580
  209.8 7.8 %copy-start.2 = (f32[24,4,16,128]{3,2,1,0:T(8,128)S(1)}, f32[24,4,16,128]{3,2,1,0:T(8,128)}, u32[]{:S(2)}) copy-start(f32[24,4,16,128]{3,2,1,0:T(8,128)} %copy-done.1) | copy-start | bytes 2359300
  209.9 8.8 %slice-start = ((f32[24,4,16,128]{3,2,1,0:T(8,128)}), f32[1,4,16,128]{3,2,1,0:T(8,128)S(1)}, s32[]{:S(2)}) async-start(f32[24,4,16,128]{3,2,1,0:T(8,128)} %copy-done.1), calls=%async_computation.5 | async-start | bytes 65536 | tf_op jit(solution)/shard_map/slice.28
  211.2 13.9 %all-to-all-start.4 = ((f32[16,4,256]{2,1,0:T(4,128)}), f32[16,4,256]{2,1,0:T(4,128)S(1)}, u32[]{:S(2)}, u32[]{:S(2)}) async-start(f32[16,4,256]{2,1,0:T(4,128)} %copy.119), calls=%async_computation.4 | async-start | bytes 131072 | tf_op jit(solution)/shard_map/all_to_all | solution.py:206
  218.8 12.8 %copy-start.15 = (pred[2048]{0:T(1024)(128)(4,1)S(1)}, pred[2048]{0:T(1024)(128)(4,1)}, u32[]{:S(2)}) copy-start(pred[2048]{0:T(1024)(128)(4,1)} %get-tuple-element.92) | copy-start | bytes 6148
